TPU v7x, 512 devices: a whole 4x4x16 slice. The times are simulated.
512 devices in a mesh: slab: 16 (over x, z_hi, core), energy: 32 (over y, z_lo).
Axes of the slice: x: 4, y: 4, z: 16 (z_hi: 2, z_lo: 8; z = z_hi * 8 + z_lo), core: 2. Of those that a mesh axis runs over, the one named last changes fastest.
Arguments:
- hamiltonian: float32 [16, 256, 256], P('slab'), may hold values from -0.375 to 0.375
- coupling: float32 [16, 256, 256], P('slab'), may hold values from -0.375 to 0.375
- pattern: int32 [16, 4, 4], P('slab'), may hold values 0 or 1
- energy: float32 [32], P('energy'), may hold values from -2 to 2
- broadening: float32 [32], P('energy'), may hold values from 0.03 to 0.1
- weights: float32 [32], P('energy'), may hold values from 0.5 to 1.5
Outputs:
- density: float32 [16, 256, 256], P('slab', 'energy')
All inputs are finite; a program needn't handle non-finite values. No bound on the sum of `pattern` on one device may be relied on, other than what follows from the above.
Results may differ from a plain program's by a relative error of at most 0.023.
Values may be sent and summed in bfloat16 or wider, within the bound.
No kernel may reach another device: no remote copies, remote signals or barrier semaphores. Data moves between devices by JAX's collectives and lax.ppermute only.
A program may use at most 64 MiB of HBM per device.

v0:
```python
import jax
import jax.numpy as jnp
from jax import lax
from jax.sharding import PartitionSpec as P

LEAD_SCALE = 0.5


def passed_along(array, axis, by):
    size = lax.axis_size(axis)
    pairs = [(i, i + by) for i in range(size) if 0 <= i + by < size]
    return lax.ppermute(array, axis, pairs)


def cut_along(array, dim, size):
    before, after = (array.shape[:dim], array.shape[dim + 1 :])
    return jnp.moveaxis(array.reshape(*before, size, -1, *after), dim, 0)


def summed_on_arrival(array, axis, dim):
    size = lax.axis_size(axis)
    parts = lax.all_to_all(cut_along(array, dim, size), axis, 0, 0, tiled=True)
    return jnp.sum(parts.astype(jnp.float32), axis=0)


def solve_green(energies, broad, ham_one, coup, handed):
    size = ham_one.shape[0]
    identity = jnp.eye(size, dtype=jnp.float32)
    sigma = jnp.einsum("ij,bpjk,lk->bpil", coup, handed, coup, precision=lax.Precision.HIGHEST)
    real_part = energies[:, None, None] * identity - ham_one - sigma[:, 0]
    imag_part = broad[:, None, None] * identity - sigma[:, 1]
    upper = jnp.concatenate([real_part, -imag_part], axis=2)
    lower = jnp.concatenate([imag_part, real_part], axis=2)
    embed = jnp.concatenate([upper, lower], axis=1)
    normal = jnp.einsum("bki,bkj->bij", embed, embed, precision=lax.Precision.HIGHEST)
    factor = jnp.linalg.cholesky(normal)
    right_side = jnp.swapaxes(upper, 1, 2)
    first = lax.linalg.triangular_solve(factor, right_side, left_side=True, lower=True)
    second = lax.linalg.triangular_solve(
        factor, first, left_side=True, lower=True, transpose_a=True
    )
    return (second[:, :size], second[:, size:])


def body(hamiltonian, coupling, pattern, energy, broadening, weights):
    local, size, _ = hamiltonian.shape
    blocks = pattern.shape[1]
    width = size // blocks
    per_device = energy.shape[0]
    tiles = jnp.broadcast_to(
        pattern.astype(jnp.float32)[:, :, None, :, None], (local, blocks, width, blocks, width)
    ).reshape(local, size, size)
    masked = coupling * tiles
    ham_sym = 0.5 * (hamiltonian + jnp.swapaxes(hamiltonian, 1, 2))
    scale = 4.0 / (per_device * lax.axis_size("energy"))
    batch_size = 1
    chain = lax.axis_size("slab")
    position = lax.axis_index("slab")
    identity = jnp.eye(size, dtype=jnp.float32)
    nothing = jnp.zeros((size, size), jnp.float32)
    lead = jnp.broadcast_to(
        jnp.stack([nothing, -LEAD_SCALE * identity]), (batch_size, 2, size, size)
    )
    empty_green = jnp.zeros((batch_size, 2, size, size), jnp.bfloat16)

    def run(operands):
        received, start = operands
        handed = jnp.where(position == 0, lead, received.astype(jnp.float32))
        real_green, imag_green = solve_green(energy, broadening, ham_sym[0], masked[0], handed)
        increments = [
            scale * jnp.einsum("b,bij->ij", weights, -imag_green, precision=lax.Precision.HIGHEST)
        ]
        rounded = jnp.stack([real_green, imag_green], axis=1).astype(jnp.bfloat16)
        return (rounded, jnp.stack(increments))

    def skip(operands):
        return (empty_green, jnp.zeros((local, size, size), jnp.float32))

    def section(step, carry):
        received, density = carry
        start = step - position
        active = jnp.logical_and(start >= 0, start < per_device)
        sent, increment = lax.cond(
            active, run, skip, (received, jnp.clip(start, 0, per_device - 1))
        )
        received = passed_along(sent, "slab", 1)
        return (received, density + increment)

    initial = (empty_green, jnp.zeros((local, size, size), jnp.float32))
    _, density = lax.fori_loop(0, chain + per_device - 1, section, initial)
    return summed_on_arrival(density.astype(jnp.bfloat16), "energy", 1)


def solution(mesh):
    in_specs = (
        P("slab", None, None),
        P("slab", None, None),
        P("slab", None, None),
        P("energy"),
        P("energy"),
        P("energy"),
    )
    out_specs = P("slab", "energy", None)
    return jax.shard_map(body, mesh=mesh, in_specs=in_specs, out_specs=out_specs, check_vma=False)
```

profile of v0, /device:TPU:262, one launch (start us, length us, event | category | flops | bytes accessed | tf_op | source)
XLA Modules:
  0.0 2436.2 jit_solution(9841753434077762182)
XLA Ops:
  3.3 2402.2 %while.18 = (s32[]{:T(128)}, bf16[1,2,256,256]{3,2,1,0:T(8,128)(2,1)S(1)}, f32[1,256,256]{2,1,0:T(8,128)}, s32[]{:T(128)}, f32[1]{0:T(128)}, /*index=5*/f32[1,25...) while((s32[]{:T(128)}, ...), condition=%wide.region_11.12_spmd.clone, body=%wide.region_0.11_spmd.clone.sunk | while | flops 3830645760 | bytes 36180680 | solution.py:90
  5.5 1.9 collective-permute-start
  7.5 1.7 select_add_fusion.2
  9.2 13.2 collective-permute-done
  23.1 1.5 conditional.3
  24.6 1.9 collective-permute-start
  26.5 1.8 select_add_fusion.2
  28.4 13.0 collective-permute-done
  43.5 1.9 collective-permute-start
  45.5 1.8 select_add_fusion.2
  47.3 12.8 collective-permute-done
  62.3 1.9 collective-permute-start
  64.2 1.8 select_add_fusion.2
  66.1 12.8 collective-permute-done
  81.1 1.9 collective-permute-start
  83.0 1.8 select_add_fusion.2
  84.8 12.8 collective-permute-done
  99.9 1.9 collective-permute-start
  101.8 1.8 select_add_fusion.2
  103.6 12.8 collective-permute-done
  118.6 1.9 collective-permute-start
  120.6 1.8 select_add_fusion.2
  122.4 12.8 collective-permute-done
  135.9 1.5 conditional.3
  137.4 1.9 collective-permute-start
  139.3 1.8 select_add_fusion.2
  141.2 12.8 collective-permute-done
  154.7 1.5 conditional.3
  156.2 1.9 collective-permute-start
  158.1 1.8 select_add_fusion.2
  159.9 12.8 collective-permute-done
  173.5 1.5 conditional.3
  175.0 1.9 collective-permute-start
  176.9 1.8 select_add_fusion.2
  178.7 12.8 collective-permute-done
  193.7 1.9 collective-permute-start
  195.7 1.8 select_add_fusion.2
  197.5 12.8 collective-permute-done
  212.5 1.9 collective-permute-start
  214.5 1.8 select_add_fusion.2
  216.3 12.8 collective-permute-done
  231.3 1.9 collective-permute-start
  233.2 1.8 select_add_fusion.2
  235.1 12.8 collective-permute-done
  250.1 1.9 collective-permute-start
  252.0 1.8 select_add_fusion.2
  253.8 1857.7 %collective-permute-done = bf16[1,2,256,256]{3,2,1,0:T(8,128)(2,1)S(1)} collective-permute-done((bf16[1,2,256,256]{3,2,1,0:T(8,128)(2,1)}, bf16[1,2,256,256]{3,2,1,0:T(8,128)(2,1)S(1)}, u32[]{:S(2)}, u32[]{:S(2)}) %collective-permute-start) | collective-permute-done | bytes 262176 | tf_op jit(solution)/shard_map/while/body/eval_jaxpr/ppermute | solution.py:12
  2112.2 142.6 %conditional.3 = (bf16[1,2,256,256]{3,2,1,0:T(8,128)(2,1)}, f32[1,256,256]{2,1,0:T(8,128)}) conditional(s32[]{:T(128)} %convert_element_type.45, () %tuple.67, (f32[1]{0:T(128)}, f32[1,256,256]{1,2,0:T(8,128)S(1)}, s32[]{:T(128)}, bf16[1,2,256,256]{3,2,1,0:T(8,128)(2,1)S(1)}, f32[1,2,256,256]{3,2,1,0:T(8,128)}, ...), branch_computations={%region_1.0_spmd, %region_2.10_spmd} | conditional | flops 3830514688 | bytes 32248196 | solution.py:83
  2115.2 1.9 fusion.12
  2117.7 11.7 custom-call.28
  2129.5 9.8 custom-call.29
  2140.1 11.7 custom-call.30
  2153.7 9.8 custom-call.31
  2164.2 11.7 custom-call.32
  2177.3 9.8 custom-call.33
  2187.7 11.7 custom-call.34
  2201.0 7.8 while.17
  2208.8 39.3 %custom-call.35 = f32[1,4,128,128]{2,3,1,0:T(8,128)S(1)} custom-call(f32[1,4,128,128]{3,2,1,0:T(8,128)S(1)} %bitcast.232), custom_call_target="InvertDiagBlocksLowerTriangular" | custom-call | tf_op jit(solution)/shard_map/while/body/eval_jaxpr/cond/branch_1_fun/triangular_solve | solution.py:39
  2254.8 1.9 collective-permute-start
  2256.8 1.8 select_add_fusion.2
  2258.6 12.8 collective-permute-done
  2273.6 130.1 %collective-permute-start = (bf16[1,2,256,256]{3,2,1,0:T(8,128)(2,1)}, bf16[1,2,256,256]{3,2,1,0:T(8,128)(2,1)S(1)}, u32[]{:S(2)}, u32[]{:S(2)}) collective-permute-start(bf16[1,2,256,256]{3,2,1,0:T(8,128)(2,1)} %get-tuple-element.379), channel_id=1, source_target_pairs={{0,32},{32,64},{64,96},{96,128},{128,160},{160,192},{192,224},{224... | collective-permute-start | bytes 786440 | tf_op jit(solution)/shard_map/while/body/eval_jaxpr/ppermute | solution.py:12
  2403.8 1.8 select_add_fusion.2
  2406.6 29.0 %all_to_all.5 = bf16[32,1,8,256]{3,2,1,0:T(8,128)(2,1)S(1)} all-to-all(bf16[32,1,8,256]{3,2,1,0:T(8,128)(2,1)S(1)} %convert_bitcast_fusion), channel_id=1, replica_groups=mesh['slab'=16,'energy'=32] {'energy'}, dimensions={0} | all-to-all | bytes 262144 | tf_op jit(solution)/shard_map/all_to_all | solution.py:22
  (189 shorter events, 76.5 us)
Async XLA Ops:
  0.0 0.7 copy-start.8
  1.2 1.0 copy-start.6
  2.3 1.0 copy-start.7
  3.4 0.7 copy-start.4
  5.5 16.9 collective-permute-start
  7.5 15.0 copy-start.5
  22.4 0.7 copy-start.4
  24.6 16.8 collective-permute-start
  26.5 14.8 copy-start.5
  41.4 0.7 copy-start.4
  43.5 16.6 collective-permute-start
  45.5 14.7 copy-start.5
  60.1 0.7 copy-start.4
  62.3 16.6 collective-permute-start
  64.2 14.7 copy-start.5
  78.9 0.7 copy-start.4
  81.1 16.6 collective-permute-start
  83.0 14.7 copy-start.5
  97.7 0.7 copy-start.4
  99.9 16.6 collective-permute-start
  101.8 14.7 copy-start.5
  116.5 0.7 copy-start.4
  118.6 16.6 collective-permute-start
  120.6 14.7 copy-start.5
  135.2 0.7 copy-start.4
  137.4 16.6 collective-permute-start
  139.3 14.7 copy-start.5
  154.0 0.7 copy-start.4
  156.2 16.6 collective-permute-start
  158.1 14.7 copy-start.5
  172.8 0.7 copy-start.4
  175.0 16.6 collective-permute-start
  176.9 14.7 copy-start.5
  191.6 0.7 copy-start.4
  193.7 16.6 collective-permute-start
  195.7 14.7 copy-start.5
  210.4 0.7 copy-start.4
  212.5 16.6 collective-permute-start
  214.4 14.7 copy-start.5
  229.1 0.7 copy-start.4
  231.3 16.6 collective-permute-start
  233.2 14.7 copy-start.5
  247.9 0.7 copy-start.4
  250.1 1861.4 %collective-permute-start = (bf16[1,2,256,256]{3,2,1,0:T(8,128)(2,1)}, bf16[1,2,256,256]{3,2,1,0:T(8,128)(2,1)S(1)}, u32[]{:S(2)}, u32[]{:S(2)}) collective-permute-start(bf16[1,2,256,256]{3,2,1,0:T(8,128)(2,1)} %get-tuple-element.379), channel_id=1, source_target_pairs={{0,32},{32,64},{64,96},{96,128},{128,160},{160,192},{192,224},{224... | collective-permute-start | bytes 786440 | tf_op jit(solution)/shard_map/while/body/eval_jaxpr/ppermute | solution.py:12
  252.0 1859.5 %copy-start.5 = (f32[1,256,256]{1,2,0:T(8,128)S(1)}, f32[1,256,256]{1,2,0:T(8,128)}, u32[]{:S(2)}) copy-start(f32[1,256,256]{1,2,0:T(8,128)} %copy-done.4) | copy-start | bytes 786436 | tf_op jit(solution)/shard_map/while
  2111.5 0.7 copy-start.4
  2115.2 1.9 copy-start
  2115.2 1.9 copy-start.2
  2200.8 47.3 %copy-start.1 = (f32[1,256,256]{1,2,0:T(8,128)S(1)}, f32[1,256,256]{1,2,0:T(8,128)}, u32[]{:S(2)}) copy-start(f32[1,256,256]{1,2,0:T(8,128)} %copy-done) | copy-start | bytes 786436 | tf_op jit(solution)/shard_map/while/body/eval_jaxpr/cond
  2200.8 47.3 %copy-start.3 = (f32[1,256,256]{1,2,0:T(8,128)S(1)}, f32[1,256,256]{1,2,0:T(8,128)}, u32[]{:S(2)}) copy-start(f32[1,256,256]{1,2,0:T(8,128)} %copy-done.2) | copy-start | bytes 786436 | tf_op jit(solution)/shard_map/while/body/eval_jaxpr/cond
  2254.8 16.6 collective-permute-start
  2256.8 14.7 copy-start.5
  2271.4 0.7 copy-start.4
  2273.6 132.0 %collective-permute-start = (bf16[1,2,256,256]{3,2,1,0:T(8,128)(2,1)}, bf16[1,2,256,256]{3,2,1,0:T(8,128)(2,1)S(1)}, u32[]{:S(2)}, u32[]{:S(2)}) collective-permute-start(bf16[1,2,256,256]{3,2,1,0:T(8,128)(2,1)} %get-tuple-element.379), channel_id=1, source_target_pairs={{0,32},{32,64},{64,96},{96,128},{128,160},{160,192},{192,224},{224... | collective-permute-start | bytes 786440 | tf_op jit(solution)/shard_map/while/body/eval_jaxpr/ppermute | solution.py:12
  2403.7 1.8 copy-start.5
where the time goes:
time: 2440 us
  waiting for transfers between devices  2040 us (84%)
  starting transfers between devices  159 us (7%)
  other arithmetic  153 us (6%)
  local copies, waits for them, and re-layouts  44.6 us (2%)
  blocking collectives  29 us (1%)
    ppermute x16, waiting for transfers between devices, passed_along(): return lax.ppermute(array, axis, pairs)  2040 us
    ppermute x16, starting transfers between devices, passed_along(): return lax.ppermute(array, axis, pairs)  159 us
    another operation x14, other arithmetic, solve_green(): factor = jnp.linalg.cholesky(normal)  78.5 us
  transfers between devices with their start and end apart: 16, of which 15 were waited for; matrix products, arithmetic and copies ran while one was open for 1% of the time, Pallas kernels for 0%

commit v1 on v0

v1 whole, which is shorter than its diff:
```python
import functools

import jax
import jax.numpy as jnp
from jax import lax
from jax.experimental import pallas as pl
from jax.experimental.pallas import tpu as pltpu
from jax.sharding import PartitionSpec as P

LEAD_SCALE = 0.5
CHUNK = 4
LINE = 8
F32=jnp.float32; BF=jnp.bfloat16
HI=lax.Precision.HIGHEST
NS=32

def eye(n, m=None):
    m = n if m is None else m
    return (lax.broadcasted_iota(jnp.int32,(n,m),0)==lax.broadcasted_iota(jnp.int32,(n,m),1)).astype(F32)

def sweep(br, bi, width):
    lanes = br.shape[1]
    two = lanes > width
    half = lax.broadcasted_iota(jnp.int32,(width,lanes),1)//width*width if two else None
    def column(x,k):
        if two:
            return jnp.take_along_axis(x, half+k, axis=1)
        return x[:,k:k+1]
    for k in range(width):
        rr = br[k:k+1,:]; ri = bi[k:k+1,:]
        cr = column(br,k); ci = column(bi,k)
        pr = cr[k:k+1,:]+1.0; pi = ci[k:k+1,:]
        den = 1.0/(pr*pr+pi*pi)
        qr = pr*den; qi = -pi*den
        sr = qr*rr-qi*ri; si = qr*ri+qi*rr
        br = br - cr*sr + ci*si
        bi = bi - cr*si - ci*sr
    return br, bi

def dot(a,b,ca,cb):
    return lax.dot_general(a,b,(((ca,),(cb,)),((),())),precision=HI,preferred_element_type=F32)

def clear(mats, off, n):
    for K in range(0,n,NS):
        rows=pl.ds(off+K,NS); cols=pl.ds(off,n)
        br = [r[rows,cols] for r,_ in mats]; bi=[i[rows,cols] for _,i in mats]
        dr = jnp.concatenate([x[:,K:K+NS] for x in br],1); di = jnp.concatenate([x[:,K:K+NS] for x in bi],1)
        dr, di = sweep(dr,di,NS)
        for j,(r,i) in enumerate(mats):
            pr = eye(NS)-dr[:,j*NS:(j+1)*NS]; pi = -di[:,j*NS:(j+1)*NS]
            left = jnp.concatenate([jnp.concatenate([pr,-pi],1),jnp.concatenate([pi,pr],1)],0)
            solved = dot(left,jnp.concatenate([br[j],bi[j]],0),1,0)
            wide = jnp.concatenate([jnp.concatenate([br[j],-bi[j]],0),jnp.concatenate([bi[j],br[j]],0)],1)
            d = dot(wide,solved,0,0)
            r[off:off+n,off:off+n] -= d[:n]
            i[off:off+n,off:off+n] -= d[n:]

def cdot(ar,ai,br,bi,ca,cb):
    lr=jnp.concatenate([ar,-ai],ca); li=jnp.concatenate([ai,ar],ca)
    right=jnp.concatenate([br,bi],cb)
    return dot(lr,right,ca,cb), dot(li,right,ca,cb)

def invert(mats):
    n = mats[0][0].shape[0]; h=n//2
    clear(mats,0,h)
    keep=[]
    for r,i in mats:
        pr=eye(h)-r[:h,:h]; pi=-i[:h,:h]
        xr=r[:h,h:]; xi=i[:h,h:]
        tr,ti=cdot(pr,pi,xr,xi,1,0)
        sr,si=cdot(xr,xi,tr,ti,0,0)
        r[h:,h:]-=sr; i[h:,h:]-=si
        keep.append((pr,pi,tr,ti))
    clear(mats,h,h)
    for (r,i),(pr,pi,tr,ti) in zip(mats,keep):
        gr=eye(h)-r[h:,h:]; gi=-i[h:,h:]
        qr,qi=cdot(tr,ti,gr,gi,1,0)
        ur,ui=cdot(qr,qi,tr,ti,1,1)
        r[:h,:h]=pr+ur; i[:h,:h]=pi+ui
        r[:h,h:]=-qr; i[:h,h:]=-qi
        r[h:,:h]=-qr.T; i[h:,:h]=-qi.T
        r[h:,h:]=gr; i[h:,h:]=gi


def bdot(a, b, ca, cb):
    return lax.dot_general(a, b, (((ca,), (cb,)), ((), ())), preferred_element_type=F32)


def split(x):
    high = x.astype(BF)
    rest = x - high.astype(F32)
    middle = rest.astype(BF)
    return high, middle, (rest - middle.astype(F32)).astype(BF)


def plane_kernel(step, pos, point, slabs, received, weighted, handed_out, ar, ai, dr, di, handed):
    active = pos[0] == step
    size = slabs.shape[-1]

    @pl.when(jnp.logical_not(active))
    def _():
        weighted[...] = jnp.zeros_like(weighted)
        handed_out[...] = jnp.zeros_like(handed_out)

    @pl.when(active)
    def _():
        if step == 0:
            handed[0] = jnp.zeros((size, size), BF)
            handed[1] = (-LEAD_SCALE * eye(size)).astype(BF)
        else:
            handed[...] = received[...]

        @pl.loop(0, CHUNK)
        def _(j):
            v = slabs[j, 1]
            for part, ref in ((0, ar), (1, ai)):
                once = bdot(v, handed[part], 1, 0)
                sigma = sum(bdot(p, v, 1, 1) for p in split(once)[::-1])
                sigma = 0.5 * (sigma + sigma.T)
                if part == 0:
                    dr[...] = point[0] * eye(size) - slabs[j, 0].astype(F32) - sigma
                    ref[...] = dr[...] - eye(size)
                else:
                    di[...] = point[1] * eye(size) - sigma
                    ref[...] = di[...]
            invert([(ar, ai)])

            @pl.loop(0, 2)
            def _(_):
                xr, xi = ar[...], ai[...]
                er, ei = cdot(dr[...], di[...], xr, xi, 1, 0)
                ur, ui = cdot(xr, xi, eye(size) - er, -ei, 1, 0)
                ar[...] = xr + ur
                ai[...] = xi + ui

            handed[0] = ar[...].astype(BF)
            handed[1] = ai[...].astype(BF)

            @pl.when(pos[1] == j)
            def _():
                weighted[...] = (point[2] * (0.0 - ai[...])).astype(weighted.dtype)

        handed_out[...] = handed[...]


def run_plane(step, pos, point, slabs, received):
    size = slabs.shape[-1]
    whole = jax.ShapeDtypeStruct((2, size, size), BF)
    return pl.pallas_call(
        functools.partial(plane_kernel, step),
        out_shape=[jax.ShapeDtypeStruct((size, size), BF), whole],
        in_specs=[pl.BlockSpec(memory_space=pltpu.SMEM)] * 2 + [pl.BlockSpec(memory_space=pltpu.VMEM)] * 2,
        out_specs=[pl.BlockSpec(memory_space=pltpu.VMEM)] * 2,
        scratch_shapes=[pltpu.VMEM((size, size), F32)] * 4 + [pltpu.VMEM((2, size, size), BF)],
        compiler_params=pltpu.CompilerParams(vmem_limit_bytes=32 * 1024 * 1024),
        cost_estimate=pl.CostEstimate(flops=400 * size**3, bytes_accessed=2 << 20, transcendentals=0),
    )(pos, point, slabs, received)


def summed_on_arrival(array, axis):
    size = lax.axis_size(axis)
    parts = lax.all_to_all(array.reshape(size, -1, array.shape[-1]), axis, 0, 0, tiled=True)
    return jnp.sum(parts.astype(F32), axis=0)


def body(hamiltonian, coupling, pattern, energy, broadening, weights):
    _, size, _ = hamiltonian.shape
    blocks = pattern.shape[1]
    width = size // blocks
    chain = lax.axis_size("slab")
    count = lax.axis_size("energy")
    tiles = jnp.broadcast_to(
        pattern[0].astype(F32)[:, None, :, None], (blocks, width, blocks, width)
    ).reshape(size, size)
    masked = coupling[0] * tiles
    ham_sym = 0.5 * (hamiltonian[0] + hamiltonian[0].T)
    own = jnp.stack([ham_sym, masked]).astype(BF)

    position = lax.axis_index("slab")
    chunk = position // CHUNK
    rank = position % CHUNK

    def flip_core(x):
        return lax.ppermute(x, "slab", [(i, i ^ 1) for i in range(chain)])

    mirrored = []
    for s in range(chain):
        for e in range(count):
            mirrored.append((s * count + e, (s ^ 2) * count + e // LINE * LINE + (LINE - 1 - e % LINE)))
    other = lax.ppermute(own, ("slab", "energy"), mirrored)
    near = flip_core(own)
    far = flip_core(other)
    even = rank % 2 == 0
    here = (jnp.where(even, own, near), jnp.where(even, near, own))
    there = (jnp.where(even, other, far), jnp.where(even, far, other))
    low = rank < 2
    slabs = jnp.stack(
        [jnp.where(low, here[0], there[0]), jnp.where(low, here[1], there[1]),
         jnp.where(low, there[0], here[0]), jnp.where(low, there[1], here[1])]
    )

    pos = jnp.stack([chunk, rank]).astype(jnp.int32)
    point = jnp.stack([energy[0], broadening[0], weights[0] * (4.0 / count)])
    received = jnp.zeros((2, size, size), BF)
    density = jnp.zeros((size, size), BF)
    for step in range(chain // CHUNK):
        weighted, handed = run_plane(step, pos, point, slabs, received)
        density = density + weighted
        if step + 1 < chain // CHUNK:
            received = lax.ppermute(
                handed, "slab", [(i, i + CHUNK) for i in range(step * CHUNK, (step + 1) * CHUNK)]
            )
    return summed_on_arrival(density, "energy")[None]


def solution(mesh):
    in_specs = (
        P("slab", None, None),
        P("slab", None, None),
        P("slab", None, None),
        P("energy"),
        P("energy"),
        P("energy"),
    )
    out_specs = P("slab", "energy", None)
    return jax.shard_map(body, mesh=mesh, in_specs=in_specs, out_specs=out_specs, check_vma=False)
```

time: 2440 us -> 660 us (0.27)
  the two profiles are of different devices: /device:TPU:262 before, /device:TPU:6 now
where the time goes in v1:
time: 660 us; the launch traced here: 651 us
  waiting for transfers between devices  454 us (69%)
  Pallas kernels  149 us (23%)
  blocking collectives  22.5 us (3%)
  starting transfers between devices  17.9 us (3%)
    ppermute x3, waiting for transfers between devices, body(): lax.ppermute(handed, 'slab', [(i, i + CHUNK) for i in range(step * CHUNK,...  433 us
    pallas_call x4, Pallas kernels, run_plane(): pl.pallas_call(functools.partial(plane_kernel, step), out_shape=[jax.Shap...  149 us
    all_to_all x1, blocking collectives, summed_on_arrival(): lax.all_to_all(array.reshape(size, -1, array.shape[-1]), axis, 0, 0, tile...  22.5 us
    ppermute x1, waiting for transfers between devices, body(): other = lax.ppermute(own, ('slab', 'energy'), mirrored)  21.2 us
  transfers between devices with their start and end apart: 6, of which 2 were waited for; matrix products, arithmetic and copies ran while one was open for 0% of the time, Pallas kernels for 0%

profile of v1, /device:TPU:6, one launch (start us, length us, event | category | flops | bytes accessed | tf_op | source)
XLA Modules:
  0.0 650.9 jit_solution(4230679960089119489)
XLA Ops:
  0.0 0.7 convert_bitcast_fusion
  0.7 0.1 broadcast_in_dim.12
  0.8 0.0 copy-start
  0.8 0.3 reshape.16
  1.2 0.6 copy-done
  1.8 0.1 copy.7
  1.9 0.0 copy-start.1
  2.0 0.9 copy-done.1
  2.9 11.4 %collective-permute-start.1 = (bf16[2,256,256]{2,1,0:T(8,128)(2,1)S(1)}, bf16[2,256,256]{2,1,0:T(8,128)(2,1)S(1)}, u32[]{:S(2)}, u32[]{:S(2)}) collective-permute-start(bf16[2,256,256]{2,1,0:T(8,128)(2,1)S(1)} %pad_maximum_fusion.1), channel_id=1, source_target_pairs={{0,71},{1,70},{2,69},{3,68},{4,67},{5,66},{6,65},{7,64},{8,79},{9,... | collective-permute-start | bytes 786440 | tf_op jit(solution)/shard_map/ppermute | solution.py:190
  14.4 1.9 collective-permute-start
  16.3 21.2 %collective-permute-done.1 = bf16[2,256,256]{2,1,0:T(8,128)(2,1)S(1)} collective-permute-done((bf16[2,256,256]{2,1,0:T(8,128)(2,1)S(1)}, bf16[2,256,256]{2,1,0:T(8,128)(2,1)S(1)}, u32[]{:S(2)}, u32[]{:S(2)}) %collective-permute-start.1) | collective-permute-done | bytes 262176 | tf_op jit(solution)/shard_map/ppermute | solution.py:190
  37.5 1.9 collective-permute-start.2
  41.4 0.1 pad_add_fusion.pos
  41.5 0.1 pad_maximum_fusion.2.point
  41.6 0.0 collective-permute-done
  41.6 0.0 collective-permute-done.2
  41.6 0.1 select_bitcast_fusion.3
  41.7 0.1 pad_maximum_fusion.slabs
  41.8 0.6 shard_map.64
  42.4 0.7 collective-permute-start.3
  43.1 0.0 collective-permute-done.3.received
  43.1 0.8 shard_map.65
  43.9 0.7 collective-permute-start.4
  44.6 0.0 collective-permute-done.4.received
  44.6 7.4 %shard_map.66 = (bf16[256,256]{1,0:T(8,128)(2,1)S(1)}, bf16[2,256,256]{2,1,0:T(8,128)(2,1)S(1)}) custom-call(s32[2]{0:T(128)S(1)} %pad_add_fusion.pos, f32[3]{0:T(128)S(1)} %pad_maximum_fusion.2.point, bf16[4,2,256,256]{3,2,1,0:T(8,128)(2,1)S(1)} %pad_maximum_fusion.slabs, bf16[2,256,256]{2,1,0:T(8,128)(2,1)S(1)} %collective-permute-done.4.received), custom_call_target="tpu_custom_call" | custom-call | flops 6710886400 | bytes 2097152 | tf_op jit(solution)/shard_map/pallas_call | solution.py:149
  52.0 1.3 collective-permute-start.5
  53.3 433.3 %collective-permute-done.5.received = bf16[2,256,256]{2,1,0:T(8,128)(2,1)S(1)} collective-permute-done((bf16[2,256,256]{2,1,0:T(8,128)(2,1)S(1)}, bf16[2,256,256]{2,1,0:T(8,128)(2,1)S(1)}, u32[]{:S(2)}, u32[]{:S(2)}) %collective-permute-start.5) | collective-permute-done | bytes 262176 | tf_op jit(solution)/shard_map/ppermute | solution.py:210
  486.5 140.8 %shard_map.67 = (bf16[256,256]{1,0:T(8,128)(2,1)S(1)}, bf16[2,256,256]{2,1,0:T(8,128)(2,1)}) custom-call(s32[2]{0:T(128)S(1)} %pad_add_fusion.pos, f32[3]{0:T(128)S(1)} %pad_maximum_fusion.2.point, bf16[4,2,256,256]{3,2,1,0:T(8,128)(2,1)S(1)} %pad_maximum_fusion.slabs, bf16[2,256,256]{2,1,0:T(8,128)(2,1)S(1)} %collective-permute-done.5.received), custom_call_target="tpu_custom_call" | custom-call | flops 6710886400 | bytes 2097152 | tf_op jit(solution)/shard_map/pallas_call | solution.py:149
  627.3 22.5 %all_to_all.5 = bf16[32,8,256]{2,1,0:T(8,128)(2,1)S(1)} all-to-all(bf16[32,8,256]{2,1,0:T(8,128)(2,1)S(1)} %add_bitcast_fusion), channel_id=1, replica_groups=mesh['slab'=16,'energy'=32] {'energy'}, dimensions={0} | all-to-all | bytes 262144 | tf_op jit(solution)/shard_map/all_to_all | solution.py:162
  649.8 0.6 convert_reduce_fusion
  (5 shorter events, 0.2 us)
Async XLA Ops:
  0.8 1.0 copy-start
  1.9 1.0 copy-start.1
  2.9 34.6 %collective-permute-start.1 = (bf16[2,256,256]{2,1,0:T(8,128)(2,1)S(1)}, bf16[2,256,256]{2,1,0:T(8,128)(2,1)S(1)}, u32[]{:S(2)}, u32[]{:S(2)}) collective-permute-start(bf16[2,256,256]{2,1,0:T(8,128)(2,1)S(1)} %pad_maximum_fusion.1), channel_id=1, source_target_pairs={{0,71},{1,70},{2,69},{3,68},{4,67},{5,66},{6,65},{7,64},{8,79},{9,... | collective-permute-start | bytes 786440 | tf_op jit(solution)/shard_map/ppermute | solution.py:190
  14.4 27.2 %collective-permute-start = (bf16[2,256,256]{2,1,0:T(8,128)(2,1)S(1)}, bf16[2,256,256]{2,1,0:T(8,128)(2,1)S(1)}, u32[]{:S(2)}, u32[]{:S(2)}) collective-permute-start(bf16[2,256,256]{2,1,0:T(8,128)(2,1)S(1)} %pad_maximum_fusion.1), channel_id=1, source_target_pairs={{0,32},{32,0},{64,96},{96,64},{128,160},{160,128},{192,224},{224,1... | collective-permute-start | bytes 786440 | tf_op jit(solution)/shard_map/ppermute | solution.py:184
  37.5 4.1 collective-permute-start.2
  42.4 0.7 collective-permute-start.3
  43.9 0.7 collective-permute-start.4
  52.0 434.6 %collective-permute-start.5 = (bf16[2,256,256]{2,1,0:T(8,128)(2,1)S(1)}, bf16[2,256,256]{2,1,0:T(8,128)(2,1)S(1)}, u32[]{:S(2)}, u32[]{:S(2)}) collective-permute-start(bf16[2,256,256]{2,1,0:T(8,128)(2,1)S(1)} %get-tuple-element.17), channel_id=1, source_target_pairs={{256,384},{288,416},{320,448},{352,480},{257,385},{289,417},{321,4... | collective-permute-start | bytes 786440 | tf_op jit(solution)/shard_map/ppermute | solution.py:210
